TPU v7x, 256 devices: a whole 4x4x8 slice. The times are simulated.
256 devices in a mesh: dp: 4 (over y), blocks: 64 (over x, z, core).
Axes of the slice: x: 4, y: 4, z: 8, core: 2. Of those that a mesh axis runs over, the one named last changes fastest.
Arguments:
- tokens: bfloat16 [16384, 8192], P('blocks', 'dp'), may hold values from -6 to 6
- dec_bias: float32 [8192], P('dp'), may hold values from -3 to 3
- routes: int32 [16384, 2], P('blocks'), may hold values from 0 to 63, all different within a row; in each aligned block of 256 rows (0 to 255, 256 to 511, ...) at most 16 rows name the same one
- latent_picks: int32 [16384, 2, 16], P('blocks'), may hold values from 0 to 1023
- enc_weight: bfloat16 [64, 8192, 1024], P('blocks', 'dp'), may hold values from -0.0625 to 0.0625
- dec_weight: bfloat16 [64, 1024, 8192], P('blocks', None, 'dp'), may hold values from -1 to 1
- enc_bias: float32 [64, 1024], P('blocks'), may hold values from -3 to 3
Outputs:
- reconstruction: bfloat16 [16384, 8192], P('blocks', 'dp')
Inputs may be any that keep to these rules, and one draw needn't show every extreme that they name: `routes`: each row names 2 different blocks; among the rows of one index of blocks no block is named by more than 16 rows, and some block by exactly 16. `latent_picks`: indices within a block; a row may name an index more than once.
All inputs are finite; a program needn't handle non-finite values.
Results may differ from a plain program's by a relative error of at most 0.0059.
Values may be sent and summed in bfloat16 or wider, within the bound.
A program may use at most 64 MiB of HBM per device.

v0:
```python
import jax
import jax.numpy as jnp
from jax import lax
from jax.sharding import PartitionSpec as P


def on_device(tokens, dec_bias, routes, latent_picks, enc_weight, dec_weight, enc_bias):
    tok_rows, quarter = tokens.shape
    top_blocks = routes.shape[1]
    pick_count = latent_picks.shape[2]
    latents = enc_weight.shape[2]
    blk_count = lax.axis_size("blocks")
    capacity = max(2, 2 * tok_rows * top_blocks // blk_count)
    slot_count = blk_count * capacity
    pair_count = tok_rows * top_blocks
    centered = (tokens.astype(jnp.float32) - dec_bias).astype(jnp.bfloat16)
    owners = routes.reshape(pair_count)
    onehot = (owners[:, None] == jnp.arange(blk_count, dtype=jnp.int32)[None, :]).astype(jnp.int32)
    slot_rank = jnp.sum(jnp.cumsum(onehot, axis=0) * onehot, axis=1) - 1
    target = owners * capacity + slot_rank
    placing = jnp.arange(slot_count, dtype=jnp.int32)[:, None] == target[None, :]
    place_half = placing.astype(jnp.bfloat16)
    paired = jnp.repeat(centered, top_blocks, axis=0)
    outgoing = jnp.dot(place_half, paired, preferred_element_type=jnp.float32).astype(jnp.bfloat16)
    outgoing = outgoing.reshape(blk_count, capacity, quarter)
    sent_picks = jnp.dot(
        placing.astype(jnp.float32),
        latent_picks.reshape(pair_count, pick_count).astype(jnp.float32),
        precision=lax.Precision.HIGHEST,
    ).astype(jnp.int32)
    sent_picks = sent_picks.reshape(blk_count, capacity, pick_count)
    enc_local = enc_weight[0]
    dec_local = dec_weight[0]
    bias_local = enc_bias[0]
    lat_ids = jnp.arange(latents, dtype=jnp.int32)
    arrived = lax.all_to_all(outgoing, "blocks", split_axis=0, concat_axis=0, tiled=True)
    chosen = lax.all_to_all(sent_picks, "blocks", split_axis=0, concat_axis=0, tiled=True)
    item_count = arrived.shape[1]
    flat_rows = arrived.reshape(blk_count * item_count, quarter)
    chosen_ids = chosen.reshape(blk_count * item_count, pick_count)
    partial_value = jnp.dot(flat_rows, enc_local, preferred_element_type=jnp.float32)
    summed = lax.psum(partial_value, "dp") + bias_local[None, :]
    keep_mask = jnp.any(chosen_ids[:, :, None] == lat_ids[None, None, :], axis=1)
    active = jnp.where(keep_mask, jnp.maximum(summed, 0.0), 0.0).astype(jnp.bfloat16)
    partial_out = jnp.dot(active, dec_local, preferred_element_type=jnp.float32).astype(
        jnp.bfloat16
    )
    partial_out = partial_out.reshape(blk_count, item_count, quarter)
    returned = lax.all_to_all(partial_out, "blocks", split_axis=0, concat_axis=0, tiled=True)
    back_rows = returned.reshape(slot_count, quarter)
    per_pair = jnp.einsum("sp,sd->pd", place_half, back_rows, preferred_element_type=jnp.float32)
    summed_out = per_pair.reshape(tok_rows, top_blocks, quarter).sum(axis=1) + dec_bias
    return summed_out.astype(jnp.bfloat16)


def solution(mesh):
    in_specs = (
        P("blocks", "dp"),
        P("dp"),
        P("blocks", None),
        P("blocks", None, None),
        P("blocks", "dp", None),
        P("blocks", None, "dp"),
        P("blocks", None),
    )
    out_specs = P("blocks", "dp")
    return jax.shard_map(
        on_device, mesh=mesh, in_specs=in_specs, out_specs=out_specs, check_vma=False
    )
```

profile of v0, /device:TPU:1, one launch (start us, length us, event | category | flops | bytes accessed | tf_op | source)
XLA Modules:
  0.0 357.7 jit_solution(9807614320305272181)
XLA Ops:
  6.5 0.0 all-reduce.2.cloned.1.call-start
  6.5 0.8 copy.23
  7.4 0.1 eq.70
  7.5 0.1 reshape.77
  7.7 1.2 reduce-window.6
  8.9 0.2 slice_reduce_fusion
  9.1 0.1 fusion.20
  9.3 1.5 subtract_convert_fusion
  10.8 1.3 broadcast_in_dim.3
  12.1 2.2 reshape.80
  14.3 3.9 %convolution_convert_fusion = bf16[1024,2048]{1,0:T(8,128)(2,1)S(1)} fusion(bf16[512,2048]{1,0:T(8,128)(2,1)} %reshape.80, s32[512]{0:T(512)S(1)} %add_add_fusion), kind=kOutput, calls=%fused_computation.7 | convolution fusion | flops 2150105088 | bytes 6293504 | tf_op jit(solution)/shard_map/dot_general | solution.py:24
  18.2 0.0 copy-start.2
  18.2 109.2 %all_to_all.15 = bf16[64,16,2048]{2,1,0:T(8,128)(2,1)S(1)} all-to-all(bf16[64,16,2048]{2,1,0:T(8,128)(2,1)S(1)} %bitcast.43), channel_id=1, replica_groups=mesh['dp'=4,'blocks'=64] {'blocks'}, dimensions={0} | all-to-all | bytes 8388608 | tf_op jit(solution)/shard_map/all_to_all | solution.py:36
  127.5 0.0 copy-done.2
  127.5 6.0 %fusion.3 = f32[1024,1024]{1,0:T(8,128)} fusion(bf16[1024,2048]{1,0:T(8,128)(2,1)S(1)} %bitcast.44, bf16[1,2048,1024]{2,1,0:T(8,128)(2,1)S(1)} %copy-done.2), kind=kOutput, calls=%fused_computation.4 | convolution fusion | flops 4294967296 | bytes 12582912 | tf_op jit(solution)/shard_map/dot_general | solution.py:41
  133.5 0.0 copy-start.1
  133.5 0.0 all-reduce.2.cloned.1.call-update
  133.6 0.7 copy-done.1
  134.3 0.0 copy-start.3
  134.3 0.1 copy.26
  134.4 1.0 fusion.16
  135.5 0.2 reshape.79
  135.7 0.3 copy.40
  136.0 0.2 reshape.87
  136.2 15.4 %all_to_all.16 = s32[64,1,256]{2,1,0:T(1,128)S(1)} all-to-all(s32[64,1,256]{2,1,0:T(1,128)S(1)} %reshape.87), channel_id=1, replica_groups=mesh['dp'=4,'blocks'=64] {'blocks'}, dimensions={0} | all-to-all | bytes 131072 | tf_op jit(solution)/shard_map/all_to_all | solution.py:37
  151.7 0.5 broadcast.47
  152.2 0.8 reduce.2
  153.0 0.2 reshape.88
  153.2 0.2 copy.31
  153.4 13.1 %fusion = pred[1024,1024]{1,0:T(8,128)(4,1)S(1)} fusion(s32[1024,16]{1,0:T(8,128)S(1)} %bitcast.45), kind=kLoop, calls=%fused_computation.1 | loop fusion | flops 32505856 | bytes 1114112 | tf_op jit(solution)/shard_map/reduce_or | solution.py:43
  166.5 61.8 %all-reduce.2.cloned.1.call-done = f32[1024,1024]{1,0:T(8,128)} async-done(((f32[1024,1024]{1,0:T(8,128)}), f32[1024,1024]{1,0:T(8,128)}) %all-reduce.2.cloned.1.call-update) | async-done | bytes 4194320 | tf_op jit(solution)/shard_map/psum | solution.py:42
  228.3 0.0 copy-done.3
  228.3 10.0 %fusion.5 = bf16[1024,2048]{1,0:T(8,128)(2,1)} fusion(bf16[1,1024,2048]{2,1,0:T(8,128)(2,1)} %param.12, pred[1024,1024]{1,0:T(8,128)(4,1)S(1)} %fusion, f32[1024,1024]{1,0:T(8,128)} %all-reduce.2.cloned.1.call-done, f32[1024]{0:T(1024)S(1)} %bitcast.49), kind=kOutput, calls=%fused_computation.8 | convolution fusion | flops 4301258752 | bytes 13635584 | tf_op jit(solution)/shard_map/dot_general | solution.py:45
  238.3 10.8 %all-to-all-start.2 = ((bf16[64,16,2048]{2,1,0:T(8,128)(2,1)}), bf16[64,16,2048]{2,1,0:T(8,128)(2,1)}, u32[]{:S(2)}, u32[]{:S(2)}) async-start(bf16[64,16,2048]{2,1,0:T(8,128)(2,1)} %bitcast.42), calls=%async_computation.2 | async-start | bytes 8388608 | tf_op jit(solution)/shard_map/all_to_all | solution.py:49
  249.1 0.4 iota_compare_fusion.4
  249.5 1.0 eq.76
  250.5 94.5 %all-to-all-done.2 = bf16[64,16,2048]{2,1,0:T(8,128)(2,1)} async-done(((bf16[64,16,2048]{2,1,0:T(8,128)(2,1)}), bf16[64,16,2048]{2,1,0:T(8,128)(2,1)}, u32[]{:S(2)}, u32[]{:S(2)}) %all-to-all-start.2) | async-done | bytes 4194336 | tf_op jit(solution)/shard_map/all_to_all | solution.py:49
  345.0 0.0 copy-start
  345.0 4.7 %fusion.13 = f32[256,2048]{1,0:T(8,128)S(1)} fusion(bf16[1024,2048,1]{1,0,2:T(8,128)(2,1)} %bitcast.10, pred[256,2,1024]{2,1,0:T(4,128)(4,1)S(1)} %eq.76), kind=kOutput, calls=%fused_computation.18 | convolution fusion | flops 2148007936 | bytes 6815744 | tf_op jit(solution)/shard_map/sp,sd->pd/dot_general | solution.py:51
  349.7 0.0 copy-done
  349.7 1.2 add_convert_fusion
  (5 shorter events, 0.1 us)
Async XLA Ops:
  6.5 221.8 %all-reduce.2.cloned.1.call-start = ((), (), s32[]{:S(2)}) async-start(), calls=%async_computation.3 | async-start | bytes 8388608 | tf_op jit(solution)/shard_map/psum | solution.py:42
  18.2 109.3 %copy-start.2 = (bf16[1,2048,1024]{2,1,0:T(8,128)(2,1)S(1)}, bf16[1,2048,1024]{2,1,0:T(8,128)(2,1)}, u32[]{:S(2)}) copy-start(bf16[1,2048,1024]{2,1,0:T(8,128)(2,1)} %param.11) | copy-start | bytes 12582916
  133.5 0.8 copy-start.1
  134.3 94.0 %copy-start.3 = (f32[1,1024]{1,0:T(1,128)S(1)}, f32[1,1024]{1,0:T(1,128)}, u32[]{:S(2)}) copy-start(f32[1,1024]{1,0:T(1,128)} %param.13) | copy-start | bytes 12292
  238.3 106.7 %all-to-all-start.2 = ((bf16[64,16,2048]{2,1,0:T(8,128)(2,1)}), bf16[64,16,2048]{2,1,0:T(8,128)(2,1)}, u32[]{:S(2)}, u32[]{:S(2)}) async-start(bf16[64,16,2048]{2,1,0:T(8,128)(2,1)} %bitcast.42), calls=%async_computation.2 | async-start | bytes 8388608 | tf_op jit(solution)/shard_map/all_to_all | solution.py:49
  345.0 4.7 %copy-start = (f32[2048]{0:T(1024)S(1)}, f32[2048]{0:T(1024)}, u32[]{:S(2)}) copy-start(f32[2048]{0:T(1024)} %param.8) | copy-start | bytes 24580
Sparse Core Ops, SparseCore 0:
  133.7 94.5 all-reduce.1
where the time goes:
time: 358 us
  waiting for transfers between devices  156 us (44%)
  blocking collectives  125 us (35%)
  matrix products  25.6 us (7%)
  other arithmetic  18.3 us (5%)
  between operations  13.6 us (4%)
  starting transfers between devices  10.8 us (3%)
  local copies, waits for them, and re-layouts  8.35 us (2%)
    all_to_all x1, blocking collectives, on_device(): lax.all_to_all(outgoing, 'blocks', split_axis=0, concat_axis=0, tiled=True)  109 us
    all_to_all x1, waiting for transfers between devices, on_device(): lax.all_to_all(partial_out, 'blocks', split_axis=0, concat_axis=0, tiled=...  94.5 us
    psum x1, waiting for transfers between devices, on_device(): summed = lax.psum(partial_value, 'dp') + bias_local[None, :]  61.8 us
    all_to_all x1, blocking collectives, on_device(): lax.all_to_all(sent_picks, 'blocks', split_axis=0, concat_axis=0, tiled=T...  15.4 us
    reduce_or x1, other arithmetic, on_device(): jnp.any(chosen_ids[:, :, None] == lat_ids[None, None, :], axis=1)  13.1 us
    all_to_all x1, starting transfers between devices, on_device(): lax.all_to_all(partial_out, 'blocks', split_axis=0, concat_axis=0, tiled=...  10.8 us
    dot_general x1, matrix products, on_device(): jnp.dot(active, dec_local, preferred_element_type=jnp.float32)  9.97 us
  transfers between devices with their start and end apart: 2, of which 2 were waited for; matrix products, arithmetic and copies ran while one was open for 5% of the time, Pallas kernels for 0%

commit v1 on v0

v1 whole, which is shorter than its diff:
```python
import functools

import jax
import jax.numpy as jnp
from jax import lax
from jax.experimental import pallas as pl
from jax.experimental.pallas import tpu as pltpu
from jax.sharding import PartitionSpec as P

F32 = jnp.float32
BF16 = jnp.bfloat16
MESH = pl.DeviceIdType.MESH
RING = 8
CORES = 2
CAP = 16
CHUNKS = 8


def dot(a, b):
    return jnp.dot(a, b, preferred_element_type=F32)


def iota(shape, axis):
    return lax.broadcasted_iota(jnp.int32, shape, axis)


def kernel(
    tok, dbias, routes, picks, ebias, enc_hbm, dec_hbm, out,
    enc, dec, cen, r1, r2, s3, r3, r4, xsa, xsb, xra, xrb, acc_a, acc_b, act_a, act_b,
    ysa, ysb, yra, yrb, b4, b3, b2, b1, t4, t3, t2, t1,
    pown, pone, ptwo, tpown, tpone, tptwo,
    tgt, tgt1, tgt2, meta, m1, m2, m3s, m3, m4, ms, mr, idx_a, idx_b,
    ya, yb, yar, ybr,
    wsem, hs, hq, us, uq, xs_sem, xq_sem, xl_sem, vs_sem, vq_sem, vl_sem,
    ms_sem, mq_sem, mx_sem, ysem_s, ysem_q,
):
    rows = tok.shape[0]
    F, _, C = cen.shape
    NP = xsa.shape[1]
    NS = NP * CAP
    HALF = NS // 2
    GA, GB = xsa.shape[2] // CAP, xsb.shape[2] // CAP
    top = routes.shape[1]
    lat = enc.shape[1]
    Y = lax.axis_size("dp")

    y = lax.axis_index("dp")
    b = lax.axis_index("blocks")
    core = lax.rem(b, CORES)
    z = lax.rem(lax.div(b, CORES), RING)
    x = lax.div(b, CORES * RING)
    me = x * CORES + core

    def block_of(p, plane):
        return (lax.div(p, CORES) * RING + plane) * CORES + lax.rem(p, CORES)

    def plane_of(step):
        return lax.rem(z + step + RING, RING)

    ahead = (block_of(me, plane_of(1)), block_of(me, plane_of(-1)))

    def to_peer(turn):
        p = lax.rem(me + turn, NP)
        return p, (y, block_of(p, z))

    def z_copy(src, dst, ssem, rsem, way):
        return pltpu.make_async_remote_copy(
            src_ref=src, dst_ref=dst, send_sem=ssem, recv_sem=rsem,
            device_id=(y, ahead[way]), device_id_type=MESH,
        )

    barrier = pltpu.get_barrier_semaphore()
    for way in range(2):
        pl.semaphore_signal(barrier, inc=1, device_id=(y, ahead[way]), device_id_type=MESH)
    for turn in range(1, NP):
        pl.semaphore_signal(barrier, inc=1, device_id=to_peer(turn)[1], device_id_type=MESH)
    for turn in range(1, Y):
        pl.semaphore_signal(
            barrier, inc=1, device_id=(lax.rem(y + turn, Y), b), device_id_type=MESH
        )
    enc_copy = pltpu.make_async_copy(enc_hbm.at[0], enc, wsem.at[0])
    dec_copy = pltpu.make_async_copy(dec_hbm.at[0], dec, wsem.at[1])
    enc_copy.start()
    dec_copy.start()
    pl.semaphore_wait(barrier, 2 + NP - 1 + Y - 1)

    def hop(h, w, f):
        src, dst = (
            (cen.at[f], r1.at[w, f]),
            (r1.at[w, f], r2.at[w, f]),
            (s3.at[w, f], r3.at[w, f]),
            (r3.at[w, f, pl.ds(NS, HALF)], r4.at[w, f]),
        )[h]
        return z_copy(src, dst, hs.at[h, w, f], hq.at[h, w, f], w)

    def back(h, w, f):
        src, dst = (
            (b1.at[w, f], t1.at[w, f]),
            (b2.at[w, f], t2.at[w, f]),
            (b3.at[w, f], t3.at[w, f]),
            (b4.at[w, f], t4.at[w, f]),
        )[h]
        return z_copy(src, dst, us.at[h, w, f], uq.at[h, w, f], 1 - w)

    def meta_hop(h, w):
        src, dst = (
            (meta, m1.at[w]),
            (m1.at[w], m2.at[w]),
            (m3s.at[w], m3.at[w]),
            (m3.at[w, pl.ds(NS, HALF)], m4.at[w]),
        )[h]
        return z_copy(src, dst, ms_sem.at[h, w], mq_sem.at[h, w], w)

    def tgt_hop(h, w):
        src, dst = ((tgt, tgt1.at[w]), (tgt1.at[w], tgt2.at[w]))[h]
        return z_copy(src, dst, ms_sem.at[4 + h, w], mq_sem.at[4 + h, w], w)

    class Exchange:
        def __init__(self, send, recv, ssem, rsem, lsem):
            self.send, self.recv, self.sems = send, recv, (ssem, rsem, lsem)

        def start(self):
            for turn in range(1, NP):
                p, device = to_peer(turn)
                pltpu.make_async_remote_copy(
                    src_ref=self.send.at[p], dst_ref=self.recv.at[me],
                    send_sem=self.sems[0], recv_sem=self.sems[1],
                    device_id=device, device_id_type=MESH,
                ).start()
            self.local().start()

        def local(self):
            return pltpu.make_async_copy(self.send.at[me], self.recv.at[me], self.sems[2])

        def both(self):
            return pltpu.make_async_remote_copy(
                src_ref=self.send.at[pl.ds(0, NP - 1)], dst_ref=self.recv.at[pl.ds(0, NP - 1)],
                send_sem=self.sems[0], recv_sem=self.sems[1],
                device_id=to_peer(1)[1], device_id_type=MESH,
            )

        def wait_recv(self):
            self.both().wait_recv()
            self.local().wait()

        def wait_send(self):
            self.both().wait_send()

    def out_a(f):
        return Exchange(xsa.at[f], xra.at[f], xs_sem.at[0, f], xq_sem.at[0, f], xl_sem.at[0, f])

    def out_b(f):
        return Exchange(xsb.at[f], xrb.at[f], xs_sem.at[1, f], xq_sem.at[1, f], xl_sem.at[1, f])

    def home_a(f):
        return Exchange(ysa.at[f], yra.at[f], vs_sem.at[0, f], vq_sem.at[0, f], vl_sem.at[0, f])

    def home_b(f):
        return Exchange(ysb.at[f], yrb.at[f], vs_sem.at[1, f], vq_sem.at[1, f], vl_sem.at[1, f])

    meta_x = Exchange(ms, mr, mx_sem.at[0], mx_sem.at[1], mx_sem.at[2])

    def y_copy(turn, src, dst, which):
        return pltpu.make_async_remote_copy(
            src_ref=src, dst_ref=dst.at[turn - 1],
            send_sem=ysem_s.at[which, turn - 1], recv_sem=ysem_q.at[which, turn - 1],
            device_id=(lax.rem(y + turn, Y), b), device_id_type=MESH,
        )

    def placing(targets, plane, first, count):
        q = iota((count, rows), 0) + first
        ids = ((lax.shift_right_logical(q, 5) * RING + plane) * CORES
               + (lax.shift_right_logical(q, 4) & 1)) * CAP + (q & (CAP - 1))
        ids = ids.astype(F32)
        return [jnp.where(targets[k:k + 1, :] == ids, 1.0, 0.0) for k in range(top)]

    def put(p_ref, t_ref, lo, kinds):
        whole = kinds[0]
        for other in kinds[1:]:
            whole = whole + other
        n = whole.shape[0]
        p_ref[lo:lo + n, :] = whole.astype(BF16)
        t_ref[:, lo:lo + n] = whole.T.astype(BF16)

    def pick_rows(kinds, source):
        total = None
        for k, one in enumerate(kinds):
            part = dot(one.astype(BF16), source).astype(BF16)
            take = (iota((128, 128), 0) == iota((128, 128), 1) + 32 * k) & (iota((128, 128), 1) < 32)
            part = dot(part, jnp.where(take, 1.0, 0.0).astype(BF16))
            total = part if total is None else total + part
        return total.astype(BF16)

    def to_peers(ref, g, value):
        ref[:, g * CAP:(g + 1) * CAP, :] = value.reshape(NP, CAP, value.shape[-1])

    def build_meta():
        lane = iota((rows, 128), 1)
        before = jnp.where(iota((rows, rows), 0) > iota((rows, rows), 1), 1.0, 0.0).astype(BF16)
        so_far = jnp.zeros((1, 128), F32)
        spread = jnp.zeros((rows, 128), F32)
        for k in range(top):
            owner = routes[:, k:k + 1]
            named = jnp.where(owner == lane, 1.0, 0.0)
            rank = jnp.sum(named * (dot(before, named.astype(BF16)) + so_far), axis=1, keepdims=True)
            so_far = so_far + jnp.sum(named, axis=0, keepdims=True)
            spread = jnp.where(lane == k, owner.astype(F32) * CAP + rank, spread)
        tgt[...] = spread.T[0:8, :]
        chosen = picks[...]
        n = chosen.shape[1]
        col, lane = iota((n, 128), 0), iota((n, 128), 1)
        base = lax.shift_right_logical(col, 4) * 32 + (col & 15)
        hi = lax.shift_right_logical(chosen, 3).astype(F32).astype(BF16)
        lo = (chosen & 7).astype(F32).astype(BF16)
        meta[...] = (
            dot(hi, jnp.where(lane == base, 1.0, 0.0).astype(BF16))
            + dot(lo, jnp.where(lane == base + 16, 1.0, 0.0).astype(BF16))
        ).astype(BF16)

    def pick_values(acc, idx, count, send):
        @pl.loop(0, count)
        def _(j):
            at = pl.ds(pl.multiple_of(j * 128, 128), 128)
            ids = idx[at, :]
            got = jnp.zeros((128, 128), F32)
            for tile in range(lat // 128):
                here = jnp.take_along_axis(
                    acc[at, tile * 128:(tile + 1) * 128], ids & 127, axis=1,
                    mode="promise_in_bounds",
                )
                got = jnp.where(lax.shift_right_logical(ids, 7) == tile, here, got)
            send[pl.ds(pl.multiple_of(j * CAP, CAP), CAP), :] = got.T[0:CAP, :]

    def spread_values(send, recv, idx, count, act):
        @pl.loop(0, count)
        def _(j):
            at = pl.ds(pl.multiple_of(j * 128, 128), 128)
            small = pl.ds(pl.multiple_of(j * CAP, CAP), CAP)
            value = send[small, :]
            for turn in range(1, Y):
                value = value + recv[turn - 1, small, :]
            value = jnp.maximum(value, 0.0)
            value = jnp.concatenate([value, jnp.zeros((128 - CAP, 128), F32)], axis=0).T
            ids = idx[at, :]
            lane = iota((32, lat), 1)
            for part in range(4):
                sub = slice(part * 32, (part + 1) * 32)
                full = jnp.zeros((32, lat), F32)
                for i in range(CAP):
                    full = jnp.where(lane == ids[sub, i:i + 1], value[sub, i:i + 1], full)
                act[pl.ds(pl.multiple_of(j * 128 + part * 32, 32), 32), :] = full.astype(BF16)

    def read_picks(mr_lo, mr_hi, idx):
        n = idx.shape[0]
        one = mr[:, mr_lo * CAP:mr_hi * CAP, :].reshape(n, 128)
        j, i = iota((128, 128), 0), iota((128, 128), 1)
        weigh = jnp.where(j == i, 8.0, jnp.where(j == i + 16, 1.0, 0.0))
        weigh = jnp.where(i < 16, weigh, 0.0).astype(BF16)
        idx[...] = dot(one, weigh).astype(jnp.int32)

    def encode(acc, value, f):
        at = pl.ds(pl.multiple_of(f * C, C), C)
        width = min(lat, 256)

        @pl.loop(0, lat // width)
        def _(n):
            cols = pl.ds(pl.multiple_of(n * width, width), width)
            acc[:, cols] += dot(value, enc[at, cols])

    def decode(act, ref, f):
        at = pl.ds(pl.multiple_of(f * C, C), C)
        value = dot(act[...], dec[:, at]).astype(BF16)
        ref[...] = value.reshape(NP, value.shape[0] // NP, C)

    scale = jnp.where(y == 0, 1.0, 0.0)
    acc_a[...] = jnp.broadcast_to(ebias[...] * scale, acc_a.shape)
    acc_b[...] = jnp.broadcast_to(ebias[...] * scale, acc_b.shape)

    @pl.loop(0, F + 5)
    def _(k):
        @pl.when(k < F)
        def _():
            cols = pl.ds(pl.multiple_of(k * C, C), C)
            cen[k] = (tok[:, cols].astype(F32) - dbias[:, cols]).astype(BF16)
            for w in range(2):
                hop(0, w, k).start()

        @pl.when(k == 0)
        def _():
            build_meta()
            for w in range(2):
                tgt_hop(0, w).start()
                meta_hop(0, w).start()
            own = placing(tgt[...], z, 0, NS)
            put(pown, tpown, 0, own)
            to_peers(ms, 0, pick_rows(own, meta[...]))
            enc_copy.wait()

        @pl.when((k >= 1) & (k <= F))
        def _():
            for w in range(2):
                hop(0, w, k - 1).wait_recv()
                hop(1, w, k - 1).start()

        @pl.when(k == 1)
        def _():
            for w in range(2):
                tgt_hop(0, w).wait_recv()
                meta_hop(0, w).wait_recv()
                tgt_hop(1, w).start()
                meta_hop(1, w).start()
                one = placing(tgt1[w], z, 0, NS)
                put(pone.at[w], tpone.at[w], 0, one)
                to_peers(ms, 1 + w, pick_rows(one, m1[w]))

        @pl.when(k == 2)
        def _():
            for w in range(2):
                step = 1 - 2 * w
                tgt_hop(1, w).wait_recv()
                meta_hop(1, w).wait_recv()
                near = placing(tgt2[w], z, 0, NS)
                put(ptwo.at[w], tptwo.at[w], 0, near)
                to_peers(ms, 3 + w, pick_rows(near, m2[w]))
                far = placing(tgt2[w], plane_of(step), 0, NS)
                put(ptwo.at[w], tptwo.at[w], NS, far)
                m3s[w, 0:NS, :] = pick_rows(far, m2[w])
                last = placing(tgt2[w], plane_of(2 * step), HALF * w, HALF)
                put(ptwo.at[w], tptwo.at[w], 2 * NS, last)
                m3s[w, NS:NS + HALF, :] = pick_rows(last, m2[w])
                meta_hop(2, w).start()

        @pl.when((k >= 2) & (k <= F + 1))
        def _():
            f = k - 2
            for w in range(2):
                hop(1, w, f).wait_recv()
                two = dot(ptwo[w], r2[w, f]).astype(BF16)
                s3[w, f] = two[NS:, :]
                hop(2, w, f).start()
                to_peers(xsa.at[f], 3 + w, two[0:NS, :])

        @pl.when((k >= 3) & (k <= F + 2))
        def _():
            f = k - 3
            for w in range(2):
                hop(2, w, f).wait_recv()
                hop(3, w, f).start()
                to_peers(xsb.at[f], w, r3[w, f, 0:NS, :])

        @pl.when(k == 3)
        def _():
            for w in range(2):
                meta_hop(2, w).wait_recv()
                meta_hop(3, w).start()
                to_peers(ms, 5 + w, m3[w, 0:NS, :])

        @pl.when((k >= 4) & (k <= F + 3))
        def _():
            f = k - 4
            for w in range(2):
                hop(3, w, f).wait_recv()
            to_peers(xsb.at[f], 2, jnp.concatenate([r4[0, f], r4[1, f]], axis=0))
            out_b(f).start()

        @pl.when(k == 4)
        def _():
            for w in range(2):
                meta_hop(3, w).wait_recv()
            to_peers(ms, 7, jnp.concatenate([m4[0], m4[1]], axis=0))
            meta_x.start()

        @pl.when((k >= 2) & (k <= F + 1))
        def _():
            f = k - 2
            to_peers(xsa.at[f], 0, dot(pown[...], cen[f]).astype(BF16))
            for w in range(2):
                to_peers(xsa.at[f], 1 + w, dot(pone[w], r1[w, f]).astype(BF16))
            out_a(f).start()

        @pl.when((k >= 3) & (k <= F + 2))
        def _():
            f = k - 3
            out_a(f).wait_recv()
            encode(acc_a, xra[f].reshape(NP * GA * CAP, C), f)

        @pl.when(k == 5)
        def _():
            meta_x.wait_recv()
            read_picks(0, GA, idx_a)
            read_picks(GA, GA + GB, idx_b)

        @pl.when(k == F + 3)
        def _():
            pick_values(acc_a, idx_a, act_a.shape[0] // 128, ya)
            for turn in range(1, Y):
                y_copy(turn, ya, yar, 0).start()
            dec_copy.wait()

        @pl.when(k == F + 4)
        def _():
            for turn in range(1, Y):
                y_copy(turn, ya, yar, 0).wait_recv()
            spread_values(ya, yar, idx_a, act_a.shape[0] // 128, act_a)

        @pl.when(k >= 5)
        def _():
            f = k - 5
            out_b(f).wait_recv()
            encode(acc_b, xrb[f].reshape(NP * GB * CAP, C), f)

    pick_values(acc_b, idx_b, act_b.shape[0] // 128, yb)
    for turn in range(1, Y):
        y_copy(turn, yb, ybr, 1).start()
    for turn in range(1, Y):
        y_copy(turn, yb, ybr, 1).wait_recv()
    spread_values(yb, ybr, idx_b, act_b.shape[0] // 128, act_b)

    def slots(ref, g):
        return ref[:, g * CAP:(g + 1) * CAP, :].reshape(NS, C)

    @pl.loop(0, F + 5)
    def _(k):
        @pl.when(k < F)
        def _():
            decode(act_b, ysb.at[k], k)
            home_b(k).start()

        @pl.when((k >= 5) & (k <= F + 4))
        def _():
            f = k - 5
            whole = dot(tpown[...], slots(yra.at[f], 0))
            for w in range(2):
                back(0, w, f).wait_recv()
                whole = whole + t1[w, f].astype(F32)
            cols = pl.ds(pl.multiple_of(f * C, C), C)
            out[:, cols] = (whole + dbias[:, cols]).astype(BF16)

        @pl.when((k >= 4) & (k <= F + 3))
        def _():
            f = k - 4
            for w in range(2):
                part = dot(tpone[w], slots(yra.at[f], 1 + w))
                back(1, w, f).wait_recv()
                b1[w, f] = (part + t2[w, f].astype(F32)).astype(BF16)
                back(0, w, f).start()

        @pl.when((k >= 3) & (k <= F + 2))
        def _():
            f = k - 3
            home_a(f).wait_recv()
            for w in range(2):
                part = dot(tptwo[w, :, 0:NS], slots(yra.at[f], 3 + w))
                back(2, w, f).wait_recv()
                part = part + dot(tptwo[w, :, NS:2 * NS], t3[w, f, 0:NS, :])
                part = part + dot(tptwo[w, :, 2 * NS:2 * NS + HALF], t3[w, f, NS:NS + HALF, :])
                b2[w, f] = part.astype(BF16)
                back(1, w, f).start()

        @pl.when((k >= 2) & (k <= F + 1))
        def _():
            f = k - 2
            for w in range(2):
                b3[w, f, 0:NS, :] = slots(yrb.at[f], w)
                back(3, w, f).wait_recv()
                b3[w, f, NS:NS + HALF, :] = t4[w, f]
                back(2, w, f).start()

        @pl.when((k >= 1) & (k <= F))
        def _():
            f = k - 1
            home_b(f).wait_recv()
            last = slots(yrb.at[f], 2)
            for w in range(2):
                b4[w, f] = last[HALF * w:HALF * (w + 1), :]
                back(3, w, f).start()
            decode(act_a, ysa.at[f], f)
            home_a(f).start()

        @pl.when(k < F)
        def _():
            for h in range(4):
                for w in range(2):
                    hop(h, w, k).wait_send()
            out_a(k).wait_send()
            out_b(k).wait_send()

        @pl.when(k >= 5)
        def _():
            for h in range(4):
                for w in range(2):
                    back(h, w, k - 5).wait_send()
            home_a(k - 5).wait_send()
            home_b(k - 5).wait_send()

    for w in range(2):
        for h in range(4):
            meta_hop(h, w).wait_send()
        for h in range(2):
            tgt_hop(h, w).wait_send()
    meta_x.wait_send()
    for turn in range(1, Y):
        y_copy(turn, ya, yar, 0).wait_send()
        y_copy(turn, yb, ybr, 1).wait_send()


def on_device(tokens, dec_bias, routes, latent_picks, enc_weight, dec_weight, enc_bias):
    rows, width = tokens.shape
    lat = enc_weight.shape[2]
    top = routes.shape[1]
    Y = lax.axis_size("dp")
    nblk = lax.axis_size("blocks")
    NP = nblk // RING
    NS = NP * CAP
    HALF = NS // 2
    F = CHUNKS
    C = width // F
    GA, GB = 5, 3
    na, nb = NP * GA * CAP, NP * GB * CAP
    V = pltpu.VMEM
    D = pltpu.SemaphoreType.DMA
    scratch = [
        V((width, lat), BF16), V((lat, width), BF16),
        V((F, rows, C), BF16), V((2, F, rows, C), BF16), V((2, F, rows, C), BF16),
        V((2, F, NS + HALF, C), BF16), V((2, F, NS + HALF, C), BF16), V((2, F, HALF, C), BF16),
        V((F, NP, GA * CAP, C), BF16), V((F, NP, GB * CAP, C), BF16),
        V((F, NP, GA * CAP, C), BF16), V((F, NP, GB * CAP, C), BF16),
        V((na, lat), F32), V((nb, lat), F32), V((na, lat), BF16), V((nb, lat), BF16),
        V((F, NP, GA * CAP, C), BF16), V((F, NP, GB * CAP, C), BF16),
        V((F, NP, GA * CAP, C), BF16), V((F, NP, GB * CAP, C), BF16),
        V((2, F, HALF, C), BF16), V((2, F, NS + HALF, C), BF16),
        V((2, F, rows, C), BF16), V((2, F, rows, C), BF16),
        V((2, F, HALF, C), BF16), V((2, F, NS + HALF, C), BF16),
        V((2, F, rows, C), BF16), V((2, F, rows, C), BF16),
        V((NS, rows), BF16), V((2, NS, rows), BF16), V((2, 2 * NS + HALF, rows), BF16),
        V((rows, NS), BF16), V((2, rows, NS), BF16), V((2, rows, 3 * NS), BF16),
        V((8, rows), F32), V((2, 8, rows), F32), V((2, 8, rows), F32),
        V((rows, 128), BF16), V((2, rows, 128), BF16), V((2, rows, 128), BF16),
        V((2, NS + HALF, 128), BF16), V((2, NS + HALF, 128), BF16), V((2, HALF, 128), BF16),
        V((NP, 8 * CAP, 128), BF16), V((NP, 8 * CAP, 128), BF16),
        V((na, 128), jnp.int32), V((nb, 128), jnp.int32),
        V((na // 128 * CAP, 128), F32), V((nb // 128 * CAP, 128), F32),
        V((max(Y - 1, 1), na // 128 * CAP, 128), F32), V((max(Y - 1, 1), nb // 128 * CAP, 128), F32),
        D((2,)), D((4, 2, F)), D((4, 2, F)), D((4, 2, F)), D((4, 2, F)),
        D((2, F)), D((2, F)), D((2, F)), D((2, F)), D((2, F)), D((2, F)),
        D((6, 2)), D((6, 2)), D((3,)), D((2, max(Y - 1, 1))), D((2, max(Y - 1, 1))),
    ]
    vmem = pl.BlockSpec(memory_space=pltpu.VMEM)
    hbm = pl.BlockSpec(memory_space=pl.ANY)
    return pl.pallas_call(
        kernel,
        out_shape=jax.ShapeDtypeStruct((rows, width), BF16),
        in_specs=[vmem] * 5 + [hbm] * 2,
        out_specs=vmem,
        scratch_shapes=scratch,
        compiler_params=pltpu.CompilerParams(
            collective_id=0, has_side_effects=True, vmem_limit_bytes=63 * 1024 * 1024
        ),
    )(
        tokens, dec_bias.reshape(1, width), routes, latent_picks.reshape(rows, -1), enc_bias,
        enc_weight, dec_weight,
    )


def solution(mesh):
    in_specs = (
        P("blocks", "dp"),
        P("dp"),
        P("blocks", None),
        P("blocks", None, None),
        P("blocks", "dp", None),
        P("blocks", None, "dp"),
        P("blocks", None),
    )
    return jax.shard_map(
        on_device, mesh=mesh, in_specs=in_specs, out_specs=P("blocks", "dp"), check_vma=False
    )
```

time: 358 us -> 208 us (0.58)
  Pallas kernels: 0 us -> 201 us
  waiting for transfers between devices: 156 us -> 0 us
  blocking collectives: 125 us -> 0 us
  matrix products: 25.6 us -> 0 us
  other arithmetic: 18.3 us -> 0 us
  between operations: 13.6 us -> 0.01 us
  starting transfers between devices: 10.8 us -> 0 us
    pallas_call x0 -> x1, Pallas kernels: none -> 201 us  [on_device(): pl.pallas_call(kernel, out_shape=jax.ShapeDtypeStruct((rows, width), BF16...]
    all_to_all x2 -> x0, blocking collectives: 125 us -> none  [the longest x1 109 us: on_device(): lax.all_to_all(outgoing, 'blocks', split_axis=0, concat_axis=0, tiled=True)]
    all_to_all x1 -> x0, waiting for transfers between devices: 94.5 us -> none  [on_device(): lax.all_to_all(partial_out, 'blocks', split_axis=0, concat_axis=0, tiled=...]
    psum x1 -> x0, waiting for transfers between devices: 61.8 us -> none  [on_device(): summed = lax.psum(partial_value, 'dp') + bias_local[None, :]]
    dot_general x5 -> x0, matrix products: 25.6 us -> none  [the longest x1 9.97 us: on_device(): jnp.dot(active, dec_local, preferred_element_type=jnp.float32)]
    reduce_or x1 -> x0, other arithmetic: 13.1 us -> none  [on_device(): jnp.any(chosen_ids[:, :, None] == lat_ids[None, None, :], axis=1)]
    all_to_all x1 -> x0, starting transfers between devices: 10.8 us -> none  [on_device(): lax.all_to_all(partial_out, 'blocks', split_axis=0, concat_axis=0, tiled=...]
  transfers between devices with their start and end apart: 2 -> 0, of which waited for: 2 -> 0; matrix products, arithmetic and copies ran while one was open for 5% -> 0% of each run, Pallas kernels for 0% -> 0%
where the time goes in v1:
time: 208 us; the launch traced here: 206 us
  Pallas kernels  201 us (97%)
  local copies, waits for them, and re-layouts  5.28 us (3%)
    pallas_call x1, Pallas kernels, on_device(): pl.pallas_call(kernel, out_shape=jax.ShapeDtypeStruct((rows, width), BF16...  201 us

profile of v1, /device:TPU:1, one launch (start us, length us, event | category | flops | bytes accessed | tf_op | source)
XLA Modules:
  0.0 205.8 jit_solution(17010333332124695742)
XLA Ops:
  0.0 1.5 copy.10.routes
  1.5 1.5 copy.11.picks
  3.0 200.5 %shard_map.73 = bf16[256,2048]{1,0:T(8,128)(2,1)} custom-call(bf16[256,2048]{1,0:T(8,128)(2,1)} %tok.1, f32[1,2048]{1,0:T(1,128)} %bitcast.3, s32[256,2]{1,0:T(8,128)} %copy.10.routes, s32[256,32]{1,0:T(8,128)} %copy.11.picks, f32[1,1024]{1,0:T(1,128)} %ebias.1, bf16[1,2048,1024]{2,1,0:T(8,128)(2,1)} %enc_hbm.1, bf16[1,1024,2048]{2,1,0:T(8,128)(2,1)} %dec_hbm.1), custom_call_target="tpu_custom_call" | custom-call | tf_op jit(solution)/shard_map/pallas_call | solution.py:550
  203.5 2.3 %copy.13 = bf16[256,2048]{1,0:T(8,128)(2,1)} copy(bf16[256,2048]{1,0:T(8,128)(2,1)} %shard_map.73) | data formatting | bytes 2097152

commit v2 on v1

v2 whole, which is shorter than its diff:
```python
import functools

import jax
import jax.numpy as jnp
from jax import lax
from jax.experimental import pallas as pl
from jax.experimental.pallas import tpu as pltpu
from jax.sharding import PartitionSpec as P

F32 = jnp.float32
BF16 = jnp.bfloat16
MESH = pl.DeviceIdType.MESH
RING = 8
CORES = 2
CAP = 16
CHUNKS = 16
HOP = 2
EARLY = 4
SWAP = 3
PARTS = 4
GROUPS = 8


def dot(a, b):
    return jnp.dot(a, b, preferred_element_type=F32)


def iota(shape, axis):
    return lax.broadcasted_iota(jnp.int32, shape, axis)


def kernel(
    tok, dbias, routes, picks, ebias, enc_hbm, dec_hbm, out,
    enc, dec, cen, r1, r2, s3, r3, r4, xs, xr, acc, act, ys, yr,
    b4, b3, b2, b1, t4, t3, t2, t1,
    pown, pone, ptwo, tpown, tpone, tptwo,
    tgt, tgt1, tgt2, meta, m1, m2, m3s, m3, m4, ms, mr, idx, yv, yg,
    wsem, hs, hq, us, uq, xs_sem, xq_sem, xl_sem, vs_sem, vq_sem, vl_sem,
    ms_sem, mq_sem, mx_sem, mr_sem, ysem_s, ysem_q,
):
    rows = tok.shape[0]
    F, _, C = cen.shape
    NP = xs.shape[1]
    NX = NP // CORES
    NS = NP * CAP
    HALF = NS // 2
    top = routes.shape[0]
    lat = enc.shape[1]
    Y = lax.axis_size("dp")

    y = lax.axis_index("dp")
    b = lax.axis_index("blocks")
    core = lax.rem(b, CORES)
    z = lax.rem(lax.div(b, CORES), RING)
    x = lax.div(b, CORES * RING)
    me = x * CORES + core

    def block_of(p, plane):
        return (lax.div(p, CORES) * RING + plane) * CORES + lax.rem(p, CORES)

    def plane_of(step):
        return lax.rem(z + step + RING, RING)

    ahead = (block_of(me, plane_of(1)), block_of(me, plane_of(-1)))
    beyond = (block_of(me, plane_of(2)), block_of(me, plane_of(-2)))

    def to_peer(turn):
        p = lax.rem(me + turn, NP)
        return p, (y, block_of(p, z))

    def z_copy(src, dst, ssem, rsem, way, far=False):
        return pltpu.make_async_remote_copy(
            src_ref=src, dst_ref=dst, send_sem=ssem, recv_sem=rsem,
            device_id=(y, (beyond if far else ahead)[way]), device_id_type=MESH,
        )

    barrier = pltpu.get_barrier_semaphore()
    for way in range(2):
        pl.semaphore_signal(barrier, inc=1, device_id=(y, ahead[way]), device_id_type=MESH)
        pl.semaphore_signal(barrier, inc=1, device_id=(y, beyond[way]), device_id_type=MESH)
    for turn in range(1, NP):
        pl.semaphore_signal(barrier, inc=1, device_id=to_peer(turn)[1], device_id_type=MESH)
    for turn in range(1, Y):
        pl.semaphore_signal(
            barrier, inc=1, device_id=(lax.rem(y + turn, Y), b), device_id_type=MESH
        )
    enc_copy = pltpu.make_async_copy(enc_hbm.at[0], enc, wsem.at[0])
    dec_copy = pltpu.make_async_copy(dec_hbm.at[0], dec, wsem.at[1])
    enc_copy.start()
    dec_copy.start()
    pl.semaphore_wait(barrier, 4 + NP - 1 + Y - 1)

    def hop(h, w, f):
        src, dst = (
            (cen.at[f], r1.at[w, f]),
            (r1.at[w, f], r2.at[w, f]),
            (s3.at[w, f, pl.ds(0, NS)], r3.at[w, f]),
            (s3.at[w, f, pl.ds(NS, HALF)], r4.at[w, f]),
        )[h]
        return z_copy(src, dst, hs.at[h, w, f], hq.at[h, w, f], w, h == 3)

    def half_cols(f):
        return pl.ds(pl.multiple_of(lax.rem(f, 2) * C, C), C)

    def part_of(f, g, p, n):
        return yr.at[lax.div(f, 2), pl.ds(p, n), pl.ds(g * CAP, CAP), half_cols(f)]

    def back(h, w, f):
        src, dst = (
            (b1.at[w, f], t1.at[w, f]),
            (b2.at[w, f], t2.at[w, f]),
            (b3.at[w, f], t3.at[w, f]),
            (b4.at[w, f], t4.at[w, f]),
        )[h]
        return z_copy(src, dst, us.at[h, w, f], uq.at[h, w, f], 1 - w, h == 3)

    def meta_hop(h, w):
        src, dst = (
            (meta, m1.at[w]),
            (m1.at[w], m2.at[w]),
            (m3s.at[w, pl.ds(0, NS)], m3.at[w]),
            (m3s.at[w, pl.ds(NS, HALF)], m4.at[w]),
        )[h]
        return z_copy(src, dst, ms_sem.at[h, w], mq_sem.at[h, w], w, h == 3)

    def tgt_hop(h, w):
        src, dst = ((tgt, tgt1.at[w]), (tgt1.at[w], tgt2.at[w]))[h]
        return z_copy(src, dst, ms_sem.at[4 + h, w], mq_sem.at[4 + h, w], w)

    class Outward:
        def __init__(self, send, landing, ssem, rsem, lsem):
            self.send, self.landing, self.sems = send, landing, (ssem, rsem, lsem)

        def local(self):
            return pltpu.make_async_copy(self.send.at[me], self.landing.at[x], self.sems[2])

        def start(self):
            for turn in range(1, NP):
                p, device = to_peer(turn)
                pltpu.make_async_remote_copy(
                    src_ref=self.send.at[p], dst_ref=self.landing.at[x],
                    send_sem=self.sems[0], recv_sem=self.sems[1],
                    device_id=device, device_id_type=MESH,
                ).start()
            self.local().start()

        def wait_send(self):
            pltpu.make_async_remote_copy(
                src_ref=self.send.at[pl.ds(0, NP - 1)], dst_ref=self.send.at[pl.ds(0, NP - 1)],
                send_sem=self.sems[0], recv_sem=self.sems[1],
                device_id=to_peer(1)[1], device_id_type=MESH,
            ).wait_send()

        def wait_recv(self, stream):
            def pieces(n):
                pltpu.make_async_remote_copy(
                    src_ref=self.landing.at[pl.ds(0, n)], dst_ref=self.landing.at[pl.ds(0, n)],
                    send_sem=self.sems[0], recv_sem=self.sems[1],
                    device_id=to_peer(1)[1], device_id_type=MESH,
                ).wait_recv()

            @pl.when(stream == core)
            def _():
                if NX > 1:
                    pieces(NX - 1)
                self.local().wait()

            @pl.when(stream != core)
            def _():
                pieces(NX)

    def outward(g):
        f = lax.rem(g, F // 2)
        return Outward(xs.at[f], xr.at[g], xs_sem.at[f], xq_sem.at[g], xl_sem.at[f])

    def outward_meta(stream):
        return Outward(ms, mr.at[stream], mx_sem.at[0], mr_sem.at[stream], mx_sem.at[1])

    def homeward(g, turn):
        f, stream = lax.rem(g, F // 2), lax.div(g, F // 2)
        to = lax.rem(x + turn, NX)
        p = to * CORES + stream
        return pltpu.make_async_remote_copy(
            src_ref=ys.at[g, to], dst_ref=yr.at[f, me],
            send_sem=vs_sem.at[g], recv_sem=vq_sem.at[f],
            device_id=(y, block_of(p, z)), device_id_type=MESH,
        )

    def homeward_local(g):
        f = lax.rem(g, F // 2)
        return pltpu.make_async_copy(ys.at[g, x], yr.at[f, me], vl_sem.at[f])

    def homeward_start(g):
        stream = lax.div(g, F // 2)
        for turn in range(1, NX):
            homeward(g, turn).start()

        @pl.when(stream == core)
        def _():
            homeward_local(g).start()

        @pl.when(stream != core)
        def _():
            homeward(g, 0).start()

    def homeward_wait_send(g):
        def pieces(n):
            pltpu.make_async_remote_copy(
                src_ref=ys.at[g, pl.ds(0, n)], dst_ref=ys.at[g, pl.ds(0, n)],
                send_sem=vs_sem.at[g], recv_sem=vq_sem.at[0],
                device_id=to_peer(1)[1], device_id_type=MESH,
            ).wait_send()

        @pl.when(lax.div(g, F // 2) == core)
        def _():
            if NX > 1:
                pieces(NX - 1)

        @pl.when(lax.div(g, F // 2) != core)
        def _():
            pieces(NX)

    def homeward_wait_recv(f):
        pltpu.make_async_remote_copy(
            src_ref=yr.at[f, pl.ds(0, NP - 1)], dst_ref=yr.at[f, pl.ds(0, NP - 1)],
            send_sem=vs_sem.at[0], recv_sem=vq_sem.at[f],
            device_id=to_peer(1)[1], device_id_type=MESH,
        ).wait_recv()
        homeward_local(core * (F // 2) + f).wait()

    part_rows = acc.shape[1] // PARTS
    part_vals = part_rows // 128 * CAP

    def y_copy(turn, stream, half):
        at = pl.ds(half * part_vals, part_vals)
        return pltpu.make_async_remote_copy(
            src_ref=yv.at[stream, at], dst_ref=yg.at[stream, turn - 1, at],
            send_sem=ysem_s.at[stream, half, turn - 1], recv_sem=ysem_q.at[stream, half, turn - 1],
            device_id=(lax.rem(y + turn, Y), b), device_id_type=MESH,
        )

    def placing(targets, plane, first, count):
        q = iota((count, rows), 0) + first
        ids = ((lax.shift_right_logical(q, 5) * RING + plane) * CORES
               + (lax.shift_right_logical(q, 4) & 1)) * CAP + (q & (CAP - 1))
        ids = ids.astype(F32)
        return [jnp.where(targets[k:k + 1, :] == ids, 1.0, 0.0) for k in range(top)]

    def put(p_ref, t_ref, lo, kinds):
        whole = kinds[0]
        for other in kinds[1:]:
            whole = whole + other
        n = whole.shape[0]
        p_ref[lo:lo + n, :] = whole.astype(BF16)
        t_ref[:, lo:lo + n] = whole.T.astype(BF16)

    def pick_rows(kinds, source):
        total = None
        for k, one in enumerate(kinds):
            part = dot(one.astype(BF16), source).astype(BF16)
            take = (iota((128, 128), 0) == iota((128, 128), 1) + 32 * k) & (iota((128, 128), 1) < 32)
            part = dot(part, jnp.where(take, 1.0, 0.0).astype(BF16))
            total = part if total is None else total + part
        return total.astype(BF16)

    def to_pair(f, g, value):
        to_peers(xs.at[lax.div(f, 2), :, :, half_cols(f)], g, value)

    def to_peers(ref, g, value):
        ref[:, g * CAP:(g + 1) * CAP, :] = value.reshape(NP, CAP, value.shape[-1])

    def build_meta():
        tgt[...] = jnp.zeros(tgt.shape, F32)
        before = jnp.where(iota((rows, rows), 0) < iota((rows, rows), 1), 1.0, 0.0).astype(BF16)
        so_far = jnp.zeros((128, 1), F32)
        for k in range(top):
            owner = routes[k:k + 1, :]
            named = jnp.where(owner == iota((128, rows), 0), 1.0, 0.0)
            rank = jnp.sum(named * (dot(named.astype(BF16), before) + so_far), axis=0, keepdims=True)
            so_far = so_far + jnp.sum(named, axis=1, keepdims=True)
            tgt[k:k + 1, :] = owner.astype(F32) * CAP + rank
        chosen = picks[...]
        n = chosen.shape[0]
        lane, col = iota((128, n), 0), iota((128, n), 1)
        base = lax.shift_right_logical(col, 4) * 32 + (col & 15)
        hi = lax.shift_right_logical(chosen, 3).astype(F32).astype(BF16)
        lo = (chosen & 7).astype(F32).astype(BF16)
        meta[...] = (
            dot(jnp.where(lane == base, 1.0, 0.0).astype(BF16), hi)
            + dot(jnp.where(lane == base + 16, 1.0, 0.0).astype(BF16), lo)
        ).T.astype(BF16)

    def pick_values(stream, half):
        @pl.loop(0, part_rows // 128)
        def _(i):
            j = half * (part_rows // 128) + i
            at = pl.ds(pl.multiple_of(j * 128, 128), 128)
            ids = idx[stream, at, :]
            got = jnp.zeros((128, 128), F32)
            for tile in range(lat // 128):
                here = jnp.take_along_axis(
                    acc[stream, at, tile * 128:(tile + 1) * 128], ids & 127, axis=1,
                    mode="promise_in_bounds",
                )
                got = jnp.where(lax.shift_right_logical(ids, 7) == tile, here, got)
            yv[stream, pl.ds(pl.multiple_of(j * CAP, CAP), CAP), :] = got.T[0:CAP, :]

    def spread_values(stream, half):
        @pl.loop(0, part_rows // 128)
        def _(i):
            j = half * (part_rows // 128) + i
            small = pl.ds(pl.multiple_of(j * CAP, CAP), CAP)
            value = yv[stream, small, :]
            for turn in range(1, Y):
                value = value + yg[stream, turn - 1, small, :]
            value = jnp.maximum(value, 0.0)
            value = jnp.concatenate([value, jnp.zeros((128 - CAP, 128), F32)], axis=0).T
            ids = idx[stream, pl.ds(pl.multiple_of(j * 128, 128), 128), :]
            lane = iota((32, lat), 1)
            for part in range(4):
                sub = slice(part * 32, (part + 1) * 32)
                full = jnp.zeros((32, lat), F32)
                for i in range(CAP):
                    full = jnp.where(lane == ids[sub, i:i + 1], value[sub, i:i + 1], full)
                at = pl.ds(pl.multiple_of(j * 128 + part * 32, 32), 32)
                act[stream, at, :] = full.astype(BF16)

    def read_picks(stream):
        one = mr[stream].reshape(acc.shape[1], 128)
        j, i = iota((128, 128), 0), iota((128, 128), 1)
        weigh = jnp.where(j == i, 8.0, jnp.where(j == i + 16, 1.0, 0.0))
        weigh = jnp.where(i < 16, weigh, 0.0).astype(BF16)
        idx[stream] = dot(one, weigh).astype(jnp.int32)

    def encode(g):
        f, stream = lax.rem(g, F // 2), lax.div(g, F // 2)
        value = xr[g].reshape(acc.shape[1], 2 * C)
        at = pl.ds(pl.multiple_of(f * 2 * C, 2 * C), 2 * C)
        width = min(lat, 256)

        @pl.loop(0, lat // width)
        def _(n):
            cols = pl.ds(pl.multiple_of(n * width, width), width)
            acc[stream, :, cols] += dot(value, enc[at, cols])

    def decode(g):
        f, stream = lax.rem(g, F // 2), lax.div(g, F // 2)
        at = pl.ds(pl.multiple_of(f * 2 * C, 2 * C), 2 * C)
        ys[g] = dot(act[stream], dec[:, at]).astype(BF16).reshape(NX, NS, 2 * C)

    def slots(f, g):
        return part_of(f, g, 0, NP)[...].reshape(NS, C)

    def within(n, count):
        return (n >= 0) & (n < count)

    encoding = 3 * HOP + SWAP
    home = max(2 * F - EARLY, F + encoding + PARTS + 1)
    ending = SWAP + 3 * HOP

    @pl.loop(0, home + 2 * F + ending + 2)
    def _(k):
        own = k - core * F

        @pl.when(within(own, F))
        def _():
            cols = pl.ds(pl.multiple_of(own * C, C), C)
            cen[own] = (tok[:, cols].astype(F32) - dbias[:, cols]).astype(BF16)
            for w in range(2):
                hop(0, w, own).start()

        @pl.when(k == 0)
        def _():
            bias = ebias[...] * jnp.where(y == 0, 1.0, 0.0)
            for stream in range(CORES):
                acc[stream] = jnp.broadcast_to(bias, acc.shape[1:])

        @pl.when(own == 0)
        def _():
            build_meta()
            for w in range(2):
                tgt_hop(0, w).start()
                meta_hop(0, w).start()
            kinds = placing(tgt[...], z, 0, NS)
            put(pown, tpown, 0, kinds)
            to_peers(ms, 0, pick_rows(kinds, meta[...]))

        @pl.when(within(own - HOP, F))
        def _():
            for w in range(2):
                hop(0, w, own - HOP).wait_recv()
                hop(1, w, own - HOP).start()

        @pl.when(own == HOP)
        def _():
            for w in range(2):
                tgt_hop(0, w).wait_recv()
                meta_hop(0, w).wait_recv()
                tgt_hop(1, w).start()
                meta_hop(1, w).start()
                kinds = placing(tgt1[w], z, 0, NS)
                put(pone.at[w], tpone.at[w], 0, kinds)
                to_peers(ms, 1 + w, pick_rows(kinds, m1[w]))

        @pl.when(own == 2 * HOP)
        def _():
            for w in range(2):
                step = 1 - 2 * w
                tgt_hop(1, w).wait_recv()
                meta_hop(1, w).wait_recv()
                near = placing(tgt2[w], z, 0, NS)
                put(ptwo.at[w], tptwo.at[w], 0, near)
                to_peers(ms, 3 + w, pick_rows(near, m2[w]))
                far = placing(tgt2[w], plane_of(step), 0, NS)
                put(ptwo.at[w], tptwo.at[w], NS, far)
                m3s[w, 0:NS, :] = pick_rows(far, m2[w])
                last = placing(tgt2[w], plane_of(2 * step), HALF * w, HALF)
                put(ptwo.at[w], tptwo.at[w], 2 * NS, last)
                m3s[w, NS:NS + HALF, :] = pick_rows(last, m2[w])
                meta_hop(2, w).start()
                meta_hop(3, w).start()

        @pl.when(within(own - 2 * HOP, F))
        def _():
            f = own - 2 * HOP
            for w in range(2):
                hop(1, w, f).wait_recv()
                two = dot(ptwo[w], r2[w, f]).astype(BF16)
                s3[w, f] = two[NS:, :]
                hop(2, w, f).start()
                hop(3, w, f).start()
                to_pair(f, 3 + w, two[0:NS, :])

        @pl.when(within(own - 3 * HOP, F))
        def _():
            f = own - 3 * HOP
            for w in range(2):
                hop(2, w, f).wait_recv()
                hop(3, w, f).wait_recv()
                to_pair(f, 5 + w, r3[w, f])
            to_pair(f, 7, jnp.concatenate([r4[0, f], r4[1, f]], axis=0))

            @pl.when(lax.rem(f, 2) == 1)
            def _():
                outward(core * (F // 2) + lax.div(f, 2)).start()

        @pl.when(own == 3 * HOP)
        def _():
            for w in range(2):
                meta_hop(2, w).wait_recv()
                meta_hop(3, w).wait_recv()
                to_peers(ms, 5 + w, m3[w])
            to_peers(ms, 7, jnp.concatenate([m4[0], m4[1]], axis=0))
            outward_meta(core).start()

        @pl.when(within(own - 2 * HOP, F))
        def _():
            f = own - 2 * HOP
            to_pair(f, 0, dot(pown[...], cen[f]).astype(BF16))
            for w in range(2):
                to_pair(f, 1 + w, dot(pone[w], r1[w, f]).astype(BF16))

        done = k - home - core * F

        @pl.when(within(done - SWAP - 2 * HOP, F))
        def _():
            f = done - SWAP - 2 * HOP
            for w in range(2):
                part = dot(tpone[w], slots(f, 1 + w))
                back(1, w, f).wait_recv()
                b1[w, f] = (part + t2[w, f].astype(F32)).astype(BF16)
                back(0, w, f).start()

        @pl.when(within(done - SWAP - HOP, F))
        def _():
            f = done - SWAP - HOP
            for w in range(2):
                part = dot(tptwo[w, :, 0:NS], slots(f, 3 + w))
                back(2, w, f).wait_recv()
                part = part + dot(tptwo[w, :, NS:2 * NS], t3[w, f])
                back(3, w, f).wait_recv()
                part = part + dot(tptwo[w, :, 2 * NS:2 * NS + HALF], t4[w, f])
                b2[w, f] = part.astype(BF16)
                back(1, w, f).start()

        @pl.when(within(done - SWAP, F))
        def _():
            f = done - SWAP

            @pl.when(lax.rem(f, 2) == 0)
            def _():
                homeward_wait_recv(lax.div(f, 2))
            last = slots(f, 7)
            for w in range(2):
                b4[w, f] = last[HALF * w:HALF * (w + 1), :]
                back(3, w, f).start()
                b3[w, f] = slots(f, 5 + w)
                back(2, w, f).start()

        @pl.when(k == 3 * HOP)
        def _():
            enc_copy.wait()
            dec_copy.wait()

        @pl.when(within(k - encoding, 2 * F) & (lax.rem(k - encoding, 2) == 1))
        def _():
            g = lax.div(k - encoding, 2)
            outward(g).wait_recv(lax.div(g, F // 2))
            encode(g)

        for stream in range(CORES):
            @pl.when(k == stream * F + encoding)
            def _():
                outward_meta(stream).wait_recv(stream)
                read_picks(stream)

        second = jnp.where(k >= 2 * F + encoding, 1, 0)
        turn_step = k - (F + encoding) - second * F

        @pl.when(within(turn_step, PARTS))
        def _():
            pick_values(second, turn_step)
            for turn in range(1, Y):
                y_copy(turn, second, turn_step).start()

        @pl.when(within(turn_step - 2, PARTS))
        def _():
            for turn in range(1, Y):
                y_copy(turn, second, turn_step - 2).wait_recv()
            spread_values(second, turn_step - 2)

        @pl.when(within(k - home, 2 * F) & (lax.rem(k - home, 2) == 0))
        def _():
            g = lax.div(k - home, 2)
            decode(g)
            homeward_start(g)

        @pl.when(within(done - ending, F))
        def _():
            f = done - ending
            whole = dot(tpown[...], slots(f, 0))
            for w in range(2):
                back(0, w, f).wait_recv()
                whole = whole + t1[w, f].astype(F32)
            cols = pl.ds(pl.multiple_of(f * C, C), C)
            out[:, cols] = (whole + dbias[:, cols]).astype(BF16)

        @pl.when(within(k - home - 3, F))
        def _():
            f = k - home - 3
            for h in range(4):
                for w in range(2):
                    hop(h, w, f).wait_send()

            @pl.when(lax.rem(f, 2) == 1)
            def _():
                outward(core * (F // 2) + lax.div(f, 2)).wait_send()

        @pl.when(within(done - ending - 1, F))
        def _():
            for h in range(4):
                for w in range(2):
                    back(h, w, done - ending - 1).wait_send()

        @pl.when(within(k - home - SWAP - 4, 2 * F) & (lax.rem(k - home - SWAP - 4, 2) == 0))
        def _():
            homeward_wait_send(lax.div(k - home - SWAP - 4, 2))

    for w in range(2):
        for h in range(4):
            meta_hop(h, w).wait_send()
        for h in range(2):
            tgt_hop(h, w).wait_send()
    outward_meta(core).wait_send()
    for stream in range(CORES):
        for half in range(PARTS):
            for turn in range(1, Y):
                y_copy(turn, stream, half).wait_send()


def on_device(tokens, dec_bias, routes, latent_picks, enc_weight, dec_weight, enc_bias):
    rows, width = tokens.shape
    lat = enc_weight.shape[2]
    Y = lax.axis_size("dp")
    nblk = lax.axis_size("blocks")
    NP = nblk // RING
    NX = NP // CORES
    NS = NP * CAP
    HALF = NS // 2
    F = CHUNKS
    C = width // F
    piece = GROUPS * CAP
    n = NX * piece
    vals = n // 128 * CAP
    V = pltpu.VMEM
    D = pltpu.SemaphoreType.DMA
    scratch = [
        V((width, lat), BF16), V((lat, width), BF16),
        V((F, rows, C), BF16), V((2, F, rows, C), BF16), V((2, F, rows, C), BF16),
        V((2, F, NS + HALF, C), BF16), V((2, F, NS, C), BF16), V((2, F, HALF, C), BF16),
        V((F // 2, NP, piece, 2 * C), BF16), V((CORES * (F // 2), NX, piece, 2 * C), BF16),
        V((CORES, n, lat), F32), V((CORES, n, lat), BF16),
        V((CORES * (F // 2), NX, piece, 2 * C), BF16), V((F // 2, NP, piece, 2 * C), BF16),
        V((2, F, HALF, C), BF16), V((2, F, NS, C), BF16),
        V((2, F, rows, C), BF16), V((2, F, rows, C), BF16),
        V((2, F, HALF, C), BF16), V((2, F, NS, C), BF16),
        V((2, F, rows, C), BF16), V((2, F, rows, C), BF16),
        V((NS, rows), BF16), V((2, NS, rows), BF16), V((2, 2 * NS + HALF, rows), BF16),
        V((rows, NS), BF16), V((2, rows, NS), BF16), V((2, rows, 3 * NS), BF16),
        V((8, rows), F32), V((2, 8, rows), F32), V((2, 8, rows), F32),
        V((rows, 128), BF16), V((2, rows, 128), BF16), V((2, rows, 128), BF16),
        V((2, NS + HALF, 128), BF16), V((2, NS, 128), BF16), V((2, HALF, 128), BF16),
        V((NP, piece, 128), BF16), V((CORES, NX, piece, 128), BF16),
        V((CORES, n, 128), jnp.int32), V((CORES, vals, 128), F32),
        V((CORES, max(Y - 1, 1), vals, 128), F32),
        D((2,)), D((4, 2, F)), D((4, 2, F)), D((4, 2, F)), D((4, 2, F)),
        D((F // 2,)), D((F,)), D((F // 2,)), D((F,)), D((F // 2,)), D((F // 2,)),
        D((6, 2)), D((6, 2)), D((2,)), D((CORES,)),
        D((CORES, PARTS, max(Y - 1, 1))), D((CORES, PARTS, max(Y - 1, 1))),
    ]
    vmem = pl.BlockSpec(memory_space=pltpu.VMEM)
    hbm = pl.BlockSpec(memory_space=pl.ANY)
    return pl.pallas_call(
        kernel,
        out_shape=jax.ShapeDtypeStruct((rows, width), BF16),
        in_specs=[vmem] * 5 + [hbm] * 2,
        out_specs=vmem,
        scratch_shapes=scratch,
        compiler_params=pltpu.CompilerParams(
            collective_id=0, has_side_effects=True, vmem_limit_bytes=63 * 1024 * 1024
        ),
    )(
        tokens, dec_bias.reshape(1, width), routes.T,
        latent_picks.transpose(1, 2, 0).reshape(-1, rows), enc_bias, enc_weight, dec_weight,
    )


def solution(mesh):
    in_specs = (
        P("blocks", "dp"),
        P("dp"),
        P("blocks", None),
        P("blocks", None, None),
        P("blocks", "dp", None),
        P("blocks", None, "dp"),
        P("blocks", None),
    )
    return jax.shard_map(
        on_device, mesh=mesh, in_specs=in_specs, out_specs=P("blocks", "dp"), check_vma=False
    )
```

time: 208 us -> 190 us (0.913); the launches traced: 206 us -> 190 us
  Pallas kernels: 201 us -> 188 us
  local copies, waits for them, and re-layouts: 5.28 us -> 2.3 us
    pallas_call x1, Pallas kernels: 201 us -> 188 us  [on_device(): pl.pallas_call(kernel, out_shape=jax.ShapeDtypeStruct((rows, width), BF16...]
where the time goes in v2:
time: 190 us
  Pallas kernels  188 us (99%)
  local copies, waits for them, and re-layouts  2.3 us (1%)
    pallas_call x1, Pallas kernels, on_device(): pl.pallas_call(kernel, out_shape=jax.ShapeDtypeStruct((rows, width), BF16...  188 us

profile of v2, /device:TPU:1, one launch (start us, length us, event | category | flops | bytes accessed | tf_op | source)
XLA Modules:
  0.0 190.0 jit_solution(1024479316523064120)
XLA Ops:
  0.0 187.7 %shard_map.73 = bf16[256,2048]{1,0:T(8,128)(2,1)} custom-call(bf16[256,2048]{1,0:T(8,128)(2,1)} %tok.1, f32[1,2048]{1,0:T(1,128)} %bitcast.6, s32[2,256]{1,0:T(2,128)} %bitcast.7, s32[32,256]{1,0:T(8,128)} %bitcast.5, f32[1,1024]{1,0:T(1,128)} %ebias.1, bf16[1,2048,1024]{2,1,0:T(8,128)(2,1)} %enc_hbm.1, bf16[1,1024,2048]{2,1,0:T(8,128)(2,1)} %dec_hbm.1), custom_call_target="tpu_custom_call" | custom-call | tf_op jit(solution)/shard_map/pallas_call | solution.py:623
  187.7 2.3 %copy.9 = bf16[256,2048]{1,0:T(8,128)(2,1)} copy(bf16[256,2048]{1,0:T(8,128)(2,1)} %shard_map.73) | data formatting | bytes 2097152

commit v3 on v2

--- a/solution.py
+++ b/solution.py
@@ -14,10 +14,12 @@
 CORES = 2
 CAP = 16
 CHUNKS = 16
-HOP = 2
+HOP = 3
+LEAD = 2
+GAP = 0
 EARLY = 4
 SWAP = 3
-PARTS = 4
+PARTS = 2
 GROUPS = 8
 
 
@@ -92,12 +94,24 @@
 
     def hop(h, w, f):
         src, dst = (
-            (cen.at[f], r1.at[w, f]),
-            (r1.at[w, f], r2.at[w, f]),
-            (s3.at[w, f, pl.ds(0, NS)], r3.at[w, f]),
-            (s3.at[w, f, pl.ds(NS, HALF)], r4.at[w, f]),
+            (cen.at[f], r1.at[f, w]),
+            (r1.at[f, w], r2.at[f, w]),
+            (s3.at[w, f, pl.ds(0, NS)], r3.at[f, w]),
+            (s3.at[w, f, pl.ds(NS, HALF)], r4.at[f, w]),
         )[h]
-        return z_copy(src, dst, hs.at[h, w, f], hq.at[h, w, f], w, h == 3)
+        return z_copy(src, dst, hs.at[h, w], hq.at[h, f], w, h == 3)
+
+    def landed(ref, sem):
+        pltpu.make_async_remote_copy(
+            src_ref=ref, dst_ref=ref, send_sem=mq_sem.at[0, 0], recv_sem=sem,
+            device_id=to_peer(1)[1], device_id_type=MESH,
+        ).wait_recv()
+
+    def hop_landed(h, f):
+        landed((r1, r2, r3, r4)[h].at[f], hq.at[h, f])
+
+    def back_landed(h, f):
+        landed((t1, t2, t3, t4)[h].at[f], uq.at[h, f])
 
     def half_cols(f):
         return pl.ds(pl.multiple_of(lax.rem(f, 2) * C, C), C)
@@ -107,12 +121,12 @@
 
     def back(h, w, f):
         src, dst = (
-            (b1.at[w, f], t1.at[w, f]),
-            (b2.at[w, f], t2.at[w, f]),
-            (b3.at[w, f], t3.at[w, f]),
-            (b4.at[w, f], t4.at[w, f]),
+            (b1.at[w, f], t1.at[f, w]),
+            (b2.at[w, f], t2.at[f, w]),
+            (b3.at[w, f], t3.at[f, w]),
+            (b4.at[w, f], t4.at[f, w]),
         )[h]
-        return z_copy(src, dst, us.at[h, w, f], uq.at[h, w, f], 1 - w, h == 3)
+        return z_copy(src, dst, us.at[h, w], uq.at[h, f], 1 - w, h == 3)
 
     def meta_hop(h, w):
         src, dst = (
@@ -144,13 +158,6 @@
                 ).start()
             self.local().start()
 
-        def wait_send(self):
-            pltpu.make_async_remote_copy(
-                src_ref=self.send.at[pl.ds(0, NP - 1)], dst_ref=self.send.at[pl.ds(0, NP - 1)],
-                send_sem=self.sems[0], recv_sem=self.sems[1],
-                device_id=to_peer(1)[1], device_id_type=MESH,
-            ).wait_send()
-
         def wait_recv(self, stream):
             def pieces(n):
                 pltpu.make_async_remote_copy(
@@ -171,7 +178,7 @@
 
     def outward(g):
         f = lax.rem(g, F // 2)
-        return Outward(xs.at[f], xr.at[g], xs_sem.at[f], xq_sem.at[g], xl_sem.at[f])
+        return Outward(xs.at[f], xr.at[g], xs_sem.at[0], xq_sem.at[g], xl_sem.at[f])
 
     def outward_meta(stream):
         return Outward(ms, mr.at[stream], mx_sem.at[0], mr_sem.at[stream], mx_sem.at[1])
@@ -182,7 +189,7 @@
         p = to * CORES + stream
         return pltpu.make_async_remote_copy(
             src_ref=ys.at[g, to], dst_ref=yr.at[f, me],
-            send_sem=vs_sem.at[g], recv_sem=vq_sem.at[f],
+            send_sem=vs_sem.at[0], recv_sem=vq_sem.at[f],
             device_id=(y, block_of(p, z)), device_id_type=MESH,
         )
 
@@ -202,23 +209,6 @@
         @pl.when(stream != core)
         def _():
             homeward(g, 0).start()
-
-    def homeward_wait_send(g):
-        def pieces(n):
-            pltpu.make_async_remote_copy(
-                src_ref=ys.at[g, pl.ds(0, n)], dst_ref=ys.at[g, pl.ds(0, n)],
-                send_sem=vs_sem.at[g], recv_sem=vq_sem.at[0],
-                device_id=to_peer(1)[1], device_id_type=MESH,
-            ).wait_send()
-
-        @pl.when(lax.div(g, F // 2) == core)
-        def _():
-            if NX > 1:
-                pieces(NX - 1)
-
-        @pl.when(lax.div(g, F // 2) != core)
-        def _():
-            pieces(NX)
 
     def homeward_wait_recv(f):
         pltpu.make_async_remote_copy(
@@ -355,27 +345,36 @@
         return (n >= 0) & (n < count)
 
     encoding = 3 * HOP + SWAP
-    home = max(2 * F - EARLY, F + encoding + PARTS + 1)
+    later = F + GAP
+    home = max(later + F - EARLY, later + encoding + PARTS)
     ending = SWAP + 3 * HOP
 
-    @pl.loop(0, home + 2 * F + ending + 2)
+    @pl.loop(0, home + 2 * F + ending)
     def _(k):
-        own = k - core * F
-
-        @pl.when(within(own, F))
-        def _():
-            cols = pl.ds(pl.multiple_of(own * C, C), C)
-            cen[own] = (tok[:, cols].astype(F32) - dbias[:, cols]).astype(BF16)
-            for w in range(2):
-                hop(0, w, own).start()
-
-        @pl.when(k == 0)
+        own = k - core * later
+
+        def depart(f):
+            cols = pl.ds(pl.multiple_of(f * C, C), C)
+            cen[f] = (tok[:, cols].astype(F32) - dbias[:, cols]).astype(BF16)
+            for w in range(2):
+                hop(0, w, f).start()
+
+        @pl.when(own == 0)
+        def _():
+            for f in range(LEAD):
+                depart(f)
+
+        @pl.when((own >= 0) & (own + LEAD < F))
+        def _():
+            depart(own + LEAD)
+
+        @pl.when(k == HOP + 1)
         def _():
             bias = ebias[...] * jnp.where(y == 0, 1.0, 0.0)
             for stream in range(CORES):
                 acc[stream] = jnp.broadcast_to(bias, acc.shape[1:])
 
-        @pl.when(own == 0)
+        @pl.when(k == 0)
         def _():
             build_meta()
             for w in range(2):
@@ -387,11 +386,11 @@
 
         @pl.when(within(own - HOP, F))
         def _():
-            for w in range(2):
-                hop(0, w, own - HOP).wait_recv()
+            hop_landed(0, own - HOP)
+            for w in range(2):
                 hop(1, w, own - HOP).start()
 
-        @pl.when(own == HOP)
+        @pl.when(k == HOP)
         def _():
             for w in range(2):
                 tgt_hop(0, w).wait_recv()
@@ -402,7 +401,7 @@
                 put(pone.at[w], tpone.at[w], 0, kinds)
                 to_peers(ms, 1 + w, pick_rows(kinds, m1[w]))
 
-        @pl.when(own == 2 * HOP)
+        @pl.when(k == 2 * HOP)
         def _():
             for w in range(2):
                 step = 1 - 2 * w
@@ -423,9 +422,9 @@
         @pl.when(within(own - 2 * HOP, F))
         def _():
             f = own - 2 * HOP
-            for w in range(2):
-                hop(1, w, f).wait_recv()
-                two = dot(ptwo[w], r2[w, f]).astype(BF16)
+            hop_landed(1, f)
+            for w in range(2):
+                two = dot(ptwo[w], r2[f, w]).astype(BF16)
                 s3[w, f] = two[NS:, :]
                 hop(2, w, f).start()
                 hop(3, w, f).start()
@@ -434,17 +433,17 @@
         @pl.when(within(own - 3 * HOP, F))
         def _():
             f = own - 3 * HOP
-            for w in range(2):
-                hop(2, w, f).wait_recv()
-                hop(3, w, f).wait_recv()
-                to_pair(f, 5 + w, r3[w, f])
-            to_pair(f, 7, jnp.concatenate([r4[0, f], r4[1, f]], axis=0))
+            hop_landed(2, f)
+            hop_landed(3, f)
+            for w in range(2):
+                to_pair(f, 5 + w, r3[f, w])
+            to_pair(f, 7, jnp.concatenate([r4[f, 0], r4[f, 1]], axis=0))
 
             @pl.when(lax.rem(f, 2) == 1)
             def _():
                 outward(core * (F // 2) + lax.div(f, 2)).start()
 
-        @pl.when(own == 3 * HOP)
+        @pl.when(k == 3 * HOP)
         def _():
             for w in range(2):
                 meta_hop(2, w).wait_recv()
@@ -458,28 +457,27 @@
             f = own - 2 * HOP
             to_pair(f, 0, dot(pown[...], cen[f]).astype(BF16))
             for w in range(2):
-                to_pair(f, 1 + w, dot(pone[w], r1[w, f]).astype(BF16))
+                to_pair(f, 1 + w, dot(pone[w], r1[f, w]).astype(BF16))
 
         done = k - home - core * F
 
         @pl.when(within(done - SWAP - 2 * HOP, F))
         def _():
             f = done - SWAP - 2 * HOP
+            back_landed(1, f)
             for w in range(2):
                 part = dot(tpone[w], slots(f, 1 + w))
-                back(1, w, f).wait_recv()
-                b1[w, f] = (part + t2[w, f].astype(F32)).astype(BF16)
+                b1[w, f] = (part + t2[f, w].astype(F32)).astype(BF16)
                 back(0, w, f).start()
 
         @pl.when(within(done - SWAP - HOP, F))
         def _():
             f = done - SWAP - HOP
-            for w in range(2):
-                part = dot(tptwo[w, :, 0:NS], slots(f, 3 + w))
-                back(2, w, f).wait_recv()
-                part = part + dot(tptwo[w, :, NS:2 * NS], t3[w, f])
-                back(3, w, f).wait_recv()
-                part = part + dot(tptwo[w, :, 2 * NS:2 * NS + HALF], t4[w, f])
+            back_landed(2, f)
+            back_landed(3, f)
+            for w in range(2):
+                every = jnp.concatenate([slots(f, 3 + w), t3[f, w], t4[f, w]], axis=0)
+                part = dot(tptwo[w, :, 0:2 * NS + HALF], every)
                 b2[w, f] = part.astype(BF16)
                 back(1, w, f).start()
 
@@ -502,20 +500,23 @@
             enc_copy.wait()
             dec_copy.wait()
 
-        @pl.when(within(k - encoding, 2 * F) & (lax.rem(k - encoding, 2) == 1))
-        def _():
-            g = lax.div(k - encoding, 2)
-            outward(g).wait_recv(lax.div(g, F // 2))
-            encode(g)
-
         for stream in range(CORES):
-            @pl.when(k == stream * F + encoding)
+            ready = k - encoding - stream * later
+
+            @pl.when(within(ready, F) & (lax.rem(ready, 2) == 1))
+            def _():
+                g = lax.div(ready, 2) + stream * (F // 2)
+                outward(g).wait_recv(stream)
+                encode(g)
+
+        for stream in range(CORES):
+            @pl.when(k == encoding + stream)
             def _():
                 outward_meta(stream).wait_recv(stream)
                 read_picks(stream)
 
-        second = jnp.where(k >= 2 * F + encoding, 1, 0)
-        turn_step = k - (F + encoding) - second * F
+        second = jnp.where(k >= later + F + encoding - 1, 1, 0)
+        turn_step = k - (F + encoding - 1) - second * later
 
         @pl.when(within(turn_step, PARTS))
         def _():
@@ -539,39 +540,31 @@
         def _():
             f = done - ending
             whole = dot(tpown[...], slots(f, 0))
-            for w in range(2):
-                back(0, w, f).wait_recv()
-                whole = whole + t1[w, f].astype(F32)
+            back_landed(0, f)
+            for w in range(2):
+                whole = whole + t1[f, w].astype(F32)
             cols = pl.ds(pl.multiple_of(f * C, C), C)
             out[:, cols] = (whole + dbias[:, cols]).astype(BF16)
 
-        @pl.when(within(k - home - 3, F))
-        def _():
-            f = k - home - 3
-            for h in range(4):
-                for w in range(2):
-                    hop(h, w, f).wait_send()
-
-            @pl.when(lax.rem(f, 2) == 1)
-            def _():
-                outward(core * (F // 2) + lax.div(f, 2)).wait_send()
-
-        @pl.when(within(done - ending - 1, F))
-        def _():
-            for h in range(4):
-                for w in range(2):
-                    back(h, w, done - ending - 1).wait_send()
-
-        @pl.when(within(k - home - SWAP - 4, 2 * F) & (lax.rem(k - home - SWAP - 4, 2) == 0))
-        def _():
-            homeward_wait_send(lax.div(k - home - SWAP - 4, 2))
-
+    def sent(ref, sem):
+        pltpu.make_async_remote_copy(
+            src_ref=ref, dst_ref=ref, send_sem=sem, recv_sem=mq_sem.at[0, 0],
+            device_id=to_peer(1)[1], device_id_type=MESH,
+        ).wait_send()
+
+    for w in range(2):
+        for h, ref in enumerate((cen, r1.at[:, w], r3.at[:, w], r4.at[:, w])):
+            sent(ref, hs.at[h, w])
+        for h, ref in enumerate((b1.at[w], b2.at[w], b3.at[w], b4.at[w])):
+            sent(ref, us.at[h, w])
+    sent(xs.at[:, pl.ds(0, NP - 1)], xs_sem.at[0])
+    sent(yr.at[:, pl.ds(0, NP - 1)], vs_sem.at[0])
     for w in range(2):
         for h in range(4):
             meta_hop(h, w).wait_send()
         for h in range(2):
             tgt_hop(h, w).wait_send()
-    outward_meta(core).wait_send()
+    sent(ms.at[pl.ds(0, NP - 1)], mx_sem.at[0])
     for stream in range(CORES):
         for half in range(PARTS):
             for turn in range(1, Y):
@@ -596,15 +589,15 @@
     D = pltpu.SemaphoreType.DMA
     scratch = [
         V((width, lat), BF16), V((lat, width), BF16),
-        V((F, rows, C), BF16), V((2, F, rows, C), BF16), V((2, F, rows, C), BF16),
-        V((2, F, NS + HALF, C), BF16), V((2, F, NS, C), BF16), V((2, F, HALF, C), BF16),
+        V((F, rows, C), BF16), V((F, 2, rows, C), BF16), V((F, 2, rows, C), BF16),
+        V((2, F, NS + HALF, C), BF16), V((F, 2, NS, C), BF16), V((F, 2, HALF, C), BF16),
         V((F // 2, NP, piece, 2 * C), BF16), V((CORES * (F // 2), NX, piece, 2 * C), BF16),
         V((CORES, n, lat), F32), V((CORES, n, lat), BF16),
         V((CORES * (F // 2), NX, piece, 2 * C), BF16), V((F // 2, NP, piece, 2 * C), BF16),
         V((2, F, HALF, C), BF16), V((2, F, NS, C), BF16),
         V((2, F, rows, C), BF16), V((2, F, rows, C), BF16),
-        V((2, F, HALF, C), BF16), V((2, F, NS, C), BF16),
-        V((2, F, rows, C), BF16), V((2, F, rows, C), BF16),
+        V((F, 2, HALF, C), BF16), V((F, 2, NS, C), BF16),
+        V((F, 2, rows, C), BF16), V((F, 2, rows, C), BF16),
         V((NS, rows), BF16), V((2, NS, rows), BF16), V((2, 2 * NS + HALF, rows), BF16),
         V((rows, NS), BF16), V((2, rows, NS), BF16), V((2, rows, 3 * NS), BF16),
         V((8, rows), F32), V((2, 8, rows), F32), V((2, 8, rows), F32),
@@ -613,8 +606,8 @@
         V((NP, piece, 128), BF16), V((CORES, NX, piece, 128), BF16),
         V((CORES, n, 128), jnp.int32), V((CORES, vals, 128), F32),
         V((CORES, max(Y - 1, 1), vals, 128), F32),
-        D((2,)), D((4, 2, F)), D((4, 2, F)), D((4, 2, F)), D((4, 2, F)),
-        D((F // 2,)), D((F,)), D((F // 2,)), D((F,)), D((F // 2,)), D((F // 2,)),
+        D((2,)), D((4, 2)), D((4, F)), D((4, 2)), D((4, F)),
+        D((1,)), D((F,)), D((F // 2,)), D((1,)), D((F // 2,)), D((F // 2,)),
         D((6, 2)), D((6, 2)), D((2,)), D((CORES,)),
         D((CORES, PARTS, max(Y - 1, 1))), D((CORES, PARTS, max(Y - 1, 1))),
     ]

time: 190 us -> 182 us (0.958)
  Pallas kernels: 188 us -> 179 us
    pallas_call x1, Pallas kernels: 188 us -> 179 us  [on_device(): pl.pallas_call(kernel, out_shape=jax.ShapeDtypeStruct((rows, width), BF16...]
where the time goes in v3:
time: 182 us; the launch traced here: 181 us
  Pallas kernels  179 us (98%)
  local copies, waits for them, and re-layouts  2.3 us (1%)
    pallas_call x1, Pallas kernels, on_device(): pl.pallas_call(kernel, out_shape=jax.ShapeDtypeStruct((rows, width), BF16...  179 us

profile of v3, /device:TPU:1, one launch (start us, length us, event | category | flops | bytes accessed | tf_op | source)
XLA Modules:
  0.0 181.5 jit_solution(18284810823239451121)
XLA Ops:
  0.0 179.2 %shard_map.73 = bf16[256,2048]{1,0:T(8,128)(2,1)} custom-call(bf16[256,2048]{1,0:T(8,128)(2,1)} %tok.1, f32[1,2048]{1,0:T(1,128)} %bitcast.6, s32[2,256]{1,0:T(2,128)} %bitcast.7, s32[32,256]{1,0:T(8,128)} %bitcast.5, f32[1,1024]{1,0:T(1,128)} %ebias.1, bf16[1,2048,1024]{2,1,0:T(8,128)(2,1)} %enc_hbm.1, bf16[1,1024,2048]{2,1,0:T(8,128)(2,1)} %dec_hbm.1), custom_call_target="tpu_custom_call" | custom-call | tf_op jit(solution)/shard_map/pallas_call | solution.py:616
  179.2 2.3 %copy.9 = bf16[256,2048]{1,0:T(8,128)(2,1)} copy(bf16[256,2048]{1,0:T(8,128)(2,1)} %shard_map.73) | data formatting | bytes 2097152

commit v4 on v3

--- a/solution.py
+++ b/solution.py
@@ -16,6 +16,7 @@
 CHUNKS = 16
 HOP = 3
 LEAD = 2
+FIRST = 1
 GAP = 0
 EARLY = 4
 SWAP = 3
@@ -344,7 +345,7 @@
     def within(n, count):
         return (n >= 0) & (n < count)
 
-    encoding = 3 * HOP + SWAP
+    encoding = FIRST + 2 * HOP + SWAP
     later = F + GAP
     home = max(later + F - EARLY, later + encoding + PARTS)
     ending = SWAP + 3 * HOP
@@ -368,7 +369,7 @@
         def _():
             depart(own + LEAD)
 
-        @pl.when(k == HOP + 1)
+        @pl.when(k == 3)
         def _():
             bias = ebias[...] * jnp.where(y == 0, 1.0, 0.0)
             for stream in range(CORES):
@@ -384,13 +385,13 @@
             put(pown, tpown, 0, kinds)
             to_peers(ms, 0, pick_rows(kinds, meta[...]))
 
-        @pl.when(within(own - HOP, F))
-        def _():
-            hop_landed(0, own - HOP)
-            for w in range(2):
-                hop(1, w, own - HOP).start()
-
-        @pl.when(k == HOP)
+        @pl.when(within(own - FIRST, F))
+        def _():
+            hop_landed(0, own - FIRST)
+            for w in range(2):
+                hop(1, w, own - FIRST).start()
+
+        @pl.when(k == 2)
         def _():
             for w in range(2):
                 tgt_hop(0, w).wait_recv()
@@ -401,7 +402,7 @@
                 put(pone.at[w], tpone.at[w], 0, kinds)
                 to_peers(ms, 1 + w, pick_rows(kinds, m1[w]))
 
-        @pl.when(k == 2 * HOP)
+        @pl.when(k == FIRST + HOP)
         def _():
             for w in range(2):
                 step = 1 - 2 * w
@@ -419,9 +420,9 @@
                 meta_hop(2, w).start()
                 meta_hop(3, w).start()
 
-        @pl.when(within(own - 2 * HOP, F))
-        def _():
-            f = own - 2 * HOP
+        @pl.when(within(own - FIRST - HOP, F))
+        def _():
+            f = own - FIRST - HOP
             hop_landed(1, f)
             for w in range(2):
                 two = dot(ptwo[w], r2[f, w]).astype(BF16)
@@ -430,9 +431,9 @@
                 hop(3, w, f).start()
                 to_pair(f, 3 + w, two[0:NS, :])
 
-        @pl.when(within(own - 3 * HOP, F))
-        def _():
-            f = own - 3 * HOP
+        @pl.when(within(own - FIRST - 2 * HOP, F))
+        def _():
+            f = own - FIRST - 2 * HOP
             hop_landed(2, f)
             hop_landed(3, f)
             for w in range(2):
@@ -443,7 +444,7 @@
             def _():
                 outward(core * (F // 2) + lax.div(f, 2)).start()
 
-        @pl.when(k == 3 * HOP)
+        @pl.when(k == FIRST + 2 * HOP)
         def _():
             for w in range(2):
                 meta_hop(2, w).wait_recv()
@@ -452,9 +453,9 @@
             to_peers(ms, 7, jnp.concatenate([m4[0], m4[1]], axis=0))
             outward_meta(core).start()
 
-        @pl.when(within(own - 2 * HOP, F))
-        def _():
-            f = own - 2 * HOP
+        @pl.when(within(own - FIRST - HOP, F))
+        def _():
+            f = own - FIRST - HOP
             to_pair(f, 0, dot(pown[...], cen[f]).astype(BF16))
             for w in range(2):
                 to_pair(f, 1 + w, dot(pone[w], r1[f, w]).astype(BF16))

time: 182 us -> 181 us (level)
  no operation moved by 1% of the time
where the time goes in v4:
time: 181 us
  Pallas kernels  179 us (99%)
  local copies, waits for them, and re-layouts  2.3 us (1%)
    pallas_call x1, Pallas kernels, on_device(): pl.pallas_call(kernel, out_shape=jax.ShapeDtypeStruct((rows, width), BF16...  179 us

profile of v4, /device:TPU:1, one launch (start us, length us, event | category | flops | bytes accessed | tf_op | source)
XLA Modules:
  0.0 180.9 jit_solution(15977925269865796865)
XLA Ops:
  0.0 178.5 %shard_map.73 = bf16[256,2048]{1,0:T(8,128)(2,1)} custom-call(bf16[256,2048]{1,0:T(8,128)(2,1)} %tok.1, f32[1,2048]{1,0:T(1,128)} %bitcast.6, s32[2,256]{1,0:T(2,128)} %bitcast.7, s32[32,256]{1,0:T(8,128)} %bitcast.5, f32[1,1024]{1,0:T(1,128)} %ebias.1, bf16[1,2048,1024]{2,1,0:T(8,128)(2,1)} %enc_hbm.1, bf16[1,1024,2048]{2,1,0:T(8,128)(2,1)} %dec_hbm.1), custom_call_target="tpu_custom_call" | custom-call | tf_op jit(solution)/shard_map/pallas_call | solution.py:617
  178.6 2.3 %copy.9 = bf16[256,2048]{1,0:T(8,128)(2,1)} copy(bf16[256,2048]{1,0:T(8,128)(2,1)} %shard_map.73) | data formatting | bytes 2097152
